TPU v7x, 512 devices: a whole 4x8x8 slice. The times are simulated.
512 devices in a mesh: side: 2 (over y_hi), grp: 8 (over z), dev: 32 (over x, y_lo, core).
Axes of the slice: x: 4, y: 8 (y_hi: 2, y_lo: 4; y = y_hi * 4 + y_lo), z: 8, core: 2. Of those that a mesh axis runs over, the one named last changes fastest.
Arguments:
- sources: float32 [2, 8, 65536], P('side', None, ('grp', 'dev')), may hold values from -2500 to 2500
- near_blocks: bfloat16 [2, 8192, 128, 128], P('side', ('grp', 'dev')), may hold values from -0.125 to 0.125
- block_rows: int32 [2, 8192], P('side', ('grp', 'dev')), may hold values from 0 to 1, as said below
- block_cols: int32 [2, 8192], P('side', ('grp', 'dev')), may hold values from 0 to 511, as said below
- mirror: int32 [65536], P(('grp', 'dev')), may hold values from 0 to 127, as said below
Outputs:
- krylov_basis: float32 [4, 2, 8, 65536], P(None, 'side', None, ('grp', 'dev'))
- hessenberg: float32 [8, 4, 3], replicated
Inputs may be any that keep to these rules, and one draw needn't show every extreme that they name: `block_rows`: in each device's aligned run of 32 entries, the first 2 are 0 to 1 in order. `block_cols`: in each device's aligned run of 32 entries, the first 2 name that device's own blocks in order, and every entry names a block of an owner at most 4 owners before or after that device (owners of a half counted in the order grp, dev); where such owners exist, some entry names a block of the owner 4 before and some one of the owner 4 after. `mirror`: each aligned run of 128 entries is a permutation of 0 to 127.
All inputs are finite; a program needn't handle non-finite values.
Results may differ from a plain program's by a relative error of at most 0.005.
Values may be sent and summed in bfloat16 or wider, within the bound.
A program may use at most 64 MiB of HBM per device.

v0:
```python
import jax
import jax.numpy as jnp
from jax import lax
from jax.sharding import PartitionSpec as P

BLOCK = 128
BLK_DEV = 2
WIN = 4
ITERS = 3
epsilon = 1e-06


def shifted(block, axis, distance):
    devices = range(lax.axis_size(axis))
    route = [(i - distance, i) for i in devices if i - distance in devices]
    return lax.ppermute(block, axis, route)


def swapped(value, axis, distance):
    return lax.ppermute(value, axis, [(i, i ^ 1 << distance) for i in range(lax.axis_size(axis))])


def on_device(sources, near_blocks, block_rows, block_cols, mirror):
    side_index = lax.axis_index("side")
    is_port = side_index == 0
    owner_index = lax.axis_index(("grp", "dev"))
    vectors = sources.shape[1]
    panels = sources.shape[2]
    total_panels = (
        1.0 * panels * lax.axis_size("side") * lax.axis_size("grp") * lax.axis_size("dev")
    )
    mirror_onehot = (
        mirror.reshape(BLK_DEV, BLOCK)[:, :, None]
        == jnp.arange(BLOCK, dtype=jnp.int32)[None, None, :]
    ).astype(jnp.float32)
    row_onehot = (block_rows[0][None, :] == jnp.arange(BLK_DEV, dtype=jnp.int32)[:, None]).astype(
        jnp.float32
    )
    window_cols = block_cols[0] - (owner_index - WIN) * BLK_DEV
    blocks = near_blocks[0]
    start = sources[0]
    inner_scale = 1.0 / total_panels
    squares = lax.psum(jnp.sum(start * start, axis=1), ("side", "grp", "dev"))
    length = jnp.sqrt(squares * inner_scale + epsilon)
    vectors_list = [start / length[:, None]]
    hessenberg = jnp.zeros((vectors, ITERS + 1, ITERS), jnp.float32)
    for column in range(ITERS):
        operator_vector = vectors_list[column]
        operator_partner = swapped(operator_vector, "side", 0)
        port_part = jnp.where(is_port, operator_vector, operator_partner)
        star_part = jnp.where(is_port, operator_partner, operator_vector)
        parity = jnp.where(is_port, 1.0, -1.0).astype(jnp.float32)
        mirrored_shaped = star_part.reshape(star_part.shape[:-1] + (BLK_DEV, BLOCK))
        field = port_part + parity * jnp.einsum(
            "bij,...bj->...bi", mirror_onehot, mirrored_shaped, precision=lax.Precision.HIGHEST
        ).reshape(star_part.shape)
        near_rounded = field.astype(jnp.bfloat16)
        below_list = []
        above_list = []
        for distance in range(1, WIN + 1):
            below_list.append(shifted(near_rounded, ("grp", "dev"), distance))
            above_list.append(shifted(near_rounded, ("grp", "dev"), -distance))
        window = jnp.concatenate(below_list[::-1] + [near_rounded] + above_list, axis=1)
        picked = window.reshape(vectors, -1, BLOCK)[:, window_cols]
        products = jnp.einsum("rkj,kij->rki", picked, blocks, preferred_element_type=jnp.float32)
        summed = jnp.einsum("bk,rki->rbi", row_onehot, products, precision=lax.Precision.HIGHEST)
        image = 0.5 * field + summed.reshape(vectors, panels)
        returned = swapped(image, "side", 0)
        symmetric = jnp.where(is_port, image, returned)
        antisym = jnp.where(is_port, returned, image)
        vector = 0.5 * (symmetric - antisym)
        shaped = vector.reshape(vector.shape[:-1] + (BLK_DEV, BLOCK))
        image = jnp.where(
            is_port,
            0.5 * (symmetric + antisym),
            jnp.einsum(
                "bij,...bi->...bj", mirror_onehot, shaped, precision=lax.Precision.HIGHEST
            ).reshape(vector.shape),
        )
        stacked = jnp.stack(vectors_list)
        products_local = jnp.sum(image[None] * stacked, axis=2)
        dot_sums = lax.psum(products_local, ("side", "grp", "dev"))
        coeffs = dot_sums * inner_scale
        remainder = image - jnp.einsum(
            "jr,jrp->rp", coeffs, stacked, precision=lax.Precision.HIGHEST
        )
        rem_squares = (
            lax.psum(jnp.sum(remainder * remainder, axis=1), ("side", "grp", "dev")) * inner_scale
        )
        rem_norm = jnp.sqrt(rem_squares + epsilon)
        vectors_list.append(remainder / rem_norm[:, None])
        hessenberg = hessenberg.at[:, : column + 1, column].set(coeffs.T)
        hessenberg = hessenberg.at[:, column + 1, column].set(rem_norm)
    final = jnp.stack(vectors_list)
    return (final[:, None], hessenberg)


def solution(mesh):
    placed = (
        P("side", None, ("grp", "dev")),
        P("side", ("grp", "dev"), None, None),
        P("side", ("grp", "dev")),
        P("side", ("grp", "dev")),
        P(("grp", "dev")),
    )
    return jax.shard_map(
        on_device,
        mesh=mesh,
        in_specs=placed,
        out_specs=(P(None, "side", None, ("grp", "dev")), P()),
        check_vma=False,
    )
```

profile of v0, /device:TPU:1, one launch (start us, length us, event | category | flops | bytes accessed | tf_op | source)
XLA Modules:
  0.0 840.6 jit_solution(13101358596570558061)
XLA Ops:
  0.7 0.9 fusion.35
  1.6 106.1 %psum.49 = f32[8]{0:T(128)S(1)} all-reduce(f32[8]{0:T(128)S(1)} %fusion.35), channel_id=1, replica_groups=mesh['side'=2,'grp'=8,'dev'=32] {'side','grp','dev'}, use_global_device_ids=true, to_apply=%region_1.0 | all-reduce | flops 8 | bytes 64 | tf_op jit(solution)/shard_map/psum | solution.py:43
  107.8 4.7 collective-permute-start
  112.5 0.6 copy-done.4
  113.2 2.9 collective-permute-done
  116.3 2.6 collective-permute-start.1
  118.9 5.9 collective-permute-start.2
  124.8 2.4 collective-permute-start.3
  127.3 2.0 collective-permute-start.4
  129.2 2.3 collective-permute-start.5
  131.6 1.3 collective-permute-start.6
  132.9 1.3 collective-permute-start.7
  134.2 1.3 collective-permute-start.8
  136.0 3.5 collective-permute-done.7
  139.5 1.4 collective-permute-done.8
  140.9 0.6 gather_fusion
  141.5 0.6 fusion.7
  142.1 0.7 copy-done.2
  143.0 5.2 collective-permute-start.9
  148.1 3.1 collective-permute-done.9
  151.6 104.0 %psum.50 = f32[1,8]{1,0:T(1,128)S(1)} all-reduce(f32[1,8]{1,0:T(1,128)S(1)} %bitcast.209), channel_id=1, replica_groups=mesh['side'=2,'grp'=8,'dev'=32] {'side','grp','dev'}, use_global_device_ids=true, to_apply=%region_3.4 | all-reduce | flops 8 | bytes 64 | tf_op jit(solution)/shard_map/psum | solution.py:82
  255.9 94.4 %psum.51 = f32[8]{0:T(128)S(1)} all-reduce(f32[8]{0:T(128)S(1)} %get-tuple-element.76), channel_id=1, replica_groups=mesh['side'=2,'grp'=8,'dev'=32] {'side','grp','dev'}, use_global_device_ids=true, to_apply=%region_5.6 | all-reduce | flops 8 | bytes 64 | tf_op jit(solution)/shard_map/psum | solution.py:88
  350.3 4.0 collective-permute-start.10
  354.4 4.3 collective-permute-done.10
  358.9 1.9 collective-permute-start.11
  360.8 7.8 collective-permute-start.12
  368.6 2.7 collective-permute-start.13
  371.3 1.9 collective-permute-start.14
  373.2 2.4 collective-permute-start.15
  375.6 1.3 collective-permute-start.16
  377.0 1.3 collective-permute-start.17
  378.3 1.3 collective-permute-start.18
  380.0 3.5 collective-permute-done.17
  383.5 1.4 collective-permute-done.18
  384.9 0.6 gather_fusion.1
  385.5 0.6 fusion.5
  386.3 4.1 collective-permute-start.19
  390.4 4.2 collective-permute-done.19
  394.9 103.1 %psum.52 = f32[2,8]{1,0:T(2,128)S(1)} all-reduce(f32[2,8]{1,0:T(2,128)S(1)} %get-tuple-element.81), channel_id=1, replica_groups=mesh['side'=2,'grp'=8,'dev'=32] {'side','grp','dev'}, use_global_device_ids=true, to_apply=%region_7.8 | all-reduce | flops 16 | bytes 128 | tf_op jit(solution)/shard_map/psum | solution.py:82
  498.4 94.2 %psum.53 = f32[8]{0:T(128)S(1)} all-reduce(f32[8]{0:T(128)S(1)} %multiply_reduce_fusion.3), channel_id=1, replica_groups=mesh['side'=2,'grp'=8,'dev'=32] {'side','grp','dev'}, use_global_device_ids=true, to_apply=%region_9.10 | all-reduce | flops 8 | bytes 64 | tf_op jit(solution)/shard_map/psum | solution.py:88
  592.7 4.7 collective-permute-start.20
  598.0 3.0 collective-permute-done.20
  601.2 2.6 collective-permute-start.21
  603.8 7.1 collective-permute-start.22
  610.9 1.5 collective-permute-start.23
  612.4 2.9 collective-permute-start.24
  615.3 1.9 collective-permute-start.25
  617.3 1.3 collective-permute-start.26
  618.6 1.3 collective-permute-start.27
  619.9 1.3 collective-permute-start.28
  621.6 4.0 collective-permute-done.27
  625.6 1.4 collective-permute-done.28
  627.6 0.6 fusion.3
  628.4 4.7 collective-permute-start.29
  633.1 0.6 fusion.86
  633.7 0.7 and_reduce_fusion
  634.4 1.3 scatter.24
  635.8 1.0 collective-permute-done.29
  637.1 104.3 %psum.54 = f32[3,8]{1,0:T(4,128)S(1)} all-reduce(f32[3,8]{1,0:T(4,128)S(1)} %get-tuple-element.79), channel_id=1, replica_groups=mesh['side'=2,'grp'=8,'dev'=32] {'side','grp','dev'}, use_global_device_ids=true, to_apply=%region_11.12 | all-reduce | flops 24 | bytes 192 | tf_op jit(solution)/shard_map/psum | solution.py:82
  741.8 94.4 %psum.55 = f32[8]{0:T(128)S(1)} all-reduce(f32[8]{0:T(128)S(1)} %multiply_reduce_fusion.2), channel_id=1, replica_groups=mesh['side'=2,'grp'=8,'dev'=32] {'side','grp','dev'}, use_global_device_ids=true, to_apply=%region_13.14 | all-reduce | flops 8 | bytes 64 | tf_op jit(solution)/shard_map/psum | solution.py:88
  836.3 0.6 maximum_bitcast_fusion
  836.9 1.8 broadcast_select_fusion
  838.7 1.3 scatter.26
  840.0 0.6 copy.9
  (95 shorter events, 6.1 us)
Async XLA Ops:
  0.6 140.8 %copy-start = (bf16[1,32,128,128]{3,2,1,0:T(8,128)(2,1)S(1)}, bf16[1,32,128,128]{3,2,1,0:T(8,128)(2,1)}, u32[]{:S(2)}) copy-start(bf16[1,32,128,128]{3,2,1,0:T(8,128)(2,1)} %param.18) | copy-start | bytes 3145732
  0.6 107.1 %copy-start.1 = (f32[1,8,256]{2,1,0:T(8,128)S(1)}, f32[1,8,256]{2,1,0:T(8,128)}, u32[]{:S(2)}) copy-start(f32[1,8,256]{2,1,0:T(8,128)} %param.17) | copy-start | bytes 24580
  107.8 8.3 collective-permute-start
  112.5 0.7 copy-start.4
  113.2 2.9 copy-start.3
  116.3 15.2 %collective-permute-start.1 = (bf16[8,256]{1,0:T(8,128)(2,1)S(1)}, bf16[8,256]{1,0:T(8,128)(2,1)S(1)}, u32[]{:S(2)}, u32[]{:S(2)}) collective-permute-start(bf16[8,256]{1,0:T(8,128)(2,1)S(1)} %get-tuple-element.98), channel_id=1, source_target_pairs={{0,4},{1,5},{2,6},{3,7},{4,8},{5,9},{6,10},{7,11},{8,12},{9,13},{1... | collective-permute-start | bytes 12296 | tf_op jit(solution)/shard_map/ppermute | solution.py:16
  118.9 14.0 %collective-permute-start.2 = (bf16[8,256]{1,0:T(8,128)(2,1)S(1)}, bf16[8,256]{1,0:T(8,128)(2,1)S(1)}, u32[]{:S(2)}, u32[]{:S(2)}) collective-permute-start(bf16[8,256]{1,0:T(8,128)(2,1)S(1)} %get-tuple-element.98), channel_id=1, source_target_pairs={{0,3},{1,4},{2,5},{3,6},{4,7},{5,8},{6,9},{7,10},{8,11},{9,12},{10... | collective-permute-start | bytes 12296 | tf_op jit(solution)/shard_map/ppermute | solution.py:16
  124.8 9.4 %collective-permute-start.3 = (bf16[8,256]{1,0:T(8,128)(2,1)S(1)}, bf16[8,256]{1,0:T(8,128)(2,1)S(1)}, u32[]{:S(2)}, u32[]{:S(2)}) collective-permute-start(bf16[8,256]{1,0:T(8,128)(2,1)S(1)} %get-tuple-element.98), channel_id=1, source_target_pairs={{0,2},{1,3},{2,4},{3,5},{4,6},{5,7},{6,8},{7,9},{8,10},{9,11},{10,... | collective-permute-start | bytes 12296 | tf_op jit(solution)/shard_map/ppermute | solution.py:16
  127.3 8.3 collective-permute-start.4
  129.2 6.4 collective-permute-start.5
  131.6 4.4 collective-permute-start.6
  132.9 6.6 collective-permute-start.7
  134.2 6.6 collective-permute-start.8
  142.1 0.7 copy-start.2
  143.0 8.3 collective-permute-start.9
  350.3 8.3 collective-permute-start.10
  358.9 16.7 %collective-permute-start.11 = (bf16[8,256]{1,0:T(8,128)(2,1)S(1)}, bf16[8,256]{1,0:T(8,128)(2,1)S(1)}, u32[]{:S(2)}, u32[]{:S(2)}) collective-permute-start(bf16[8,256]{1,0:T(8,128)(2,1)S(1)} %get-tuple-element.102), channel_id=1, source_target_pairs={{0,4},{1,5},{2,6},{3,7},{4,8},{5,9},{6,10},{7,11},{8,12},{9,13},{1... | collective-permute-start | bytes 12296 | tf_op jit(solution)/shard_map/ppermute | solution.py:16
  360.8 16.2 %collective-permute-start.12 = (bf16[8,256]{1,0:T(8,128)(2,1)S(1)}, bf16[8,256]{1,0:T(8,128)(2,1)S(1)}, u32[]{:S(2)}, u32[]{:S(2)}) collective-permute-start(bf16[8,256]{1,0:T(8,128)(2,1)S(1)} %get-tuple-element.102), channel_id=1, source_target_pairs={{0,3},{1,4},{2,5},{3,6},{4,7},{5,8},{6,9},{7,10},{8,11},{9,12},{10... | collective-permute-start | bytes 12296 | tf_op jit(solution)/shard_map/ppermute | solution.py:16
  368.6 9.7 %collective-permute-start.13 = (bf16[8,256]{1,0:T(8,128)(2,1)S(1)}, bf16[8,256]{1,0:T(8,128)(2,1)S(1)}, u32[]{:S(2)}, u32[]{:S(2)}) collective-permute-start(bf16[8,256]{1,0:T(8,128)(2,1)S(1)} %get-tuple-element.102), channel_id=1, source_target_pairs={{0,2},{1,3},{2,4},{3,5},{4,6},{5,7},{6,8},{7,9},{8,10},{9,11},{10,... | collective-permute-start | bytes 12296 | tf_op jit(solution)/shard_map/ppermute | solution.py:16
  371.3 8.3 collective-permute-start.14
  373.2 6.4 collective-permute-start.15
  375.6 4.4 collective-permute-start.16
  377.0 6.5 collective-permute-start.17
  378.3 6.6 collective-permute-start.18
  386.3 8.3 collective-permute-start.19
  592.7 8.3 collective-permute-start.20
  601.2 16.1 %collective-permute-start.21 = (bf16[8,256]{1,0:T(8,128)(2,1)S(1)}, bf16[8,256]{1,0:T(8,128)(2,1)S(1)}, u32[]{:S(2)}, u32[]{:S(2)}) collective-permute-start(bf16[8,256]{1,0:T(8,128)(2,1)S(1)} %get-tuple-element.104), channel_id=1, source_target_pairs={{0,4},{1,5},{2,6},{3,7},{4,8},{5,9},{6,10},{7,11},{8,12},{9,13},{1... | collective-permute-start | bytes 12296 | tf_op jit(solution)/shard_map/ppermute | solution.py:16
  603.8 14.8 %collective-permute-start.22 = (bf16[8,256]{1,0:T(8,128)(2,1)S(1)}, bf16[8,256]{1,0:T(8,128)(2,1)S(1)}, u32[]{:S(2)}, u32[]{:S(2)}) collective-permute-start(bf16[8,256]{1,0:T(8,128)(2,1)S(1)} %get-tuple-element.104), channel_id=1, source_target_pairs={{0,3},{1,4},{2,5},{3,6},{4,7},{5,8},{6,9},{7,10},{8,11},{9,12},{10... | collective-permute-start | bytes 12296 | tf_op jit(solution)/shard_map/ppermute | solution.py:16
  610.9 9.0 %collective-permute-start.23 = (bf16[8,256]{1,0:T(8,128)(2,1)S(1)}, bf16[8,256]{1,0:T(8,128)(2,1)S(1)}, u32[]{:S(2)}, u32[]{:S(2)}) collective-permute-start(bf16[8,256]{1,0:T(8,128)(2,1)S(1)} %get-tuple-element.104), channel_id=1, source_target_pairs={{0,2},{1,3},{2,4},{3,5},{4,6},{5,7},{6,8},{7,9},{8,10},{9,11},{10,... | collective-permute-start | bytes 12296 | tf_op jit(solution)/shard_map/ppermute | solution.py:16
  612.4 8.8 %collective-permute-start.24 = (bf16[8,256]{1,0:T(8,128)(2,1)S(1)}, bf16[8,256]{1,0:T(8,128)(2,1)S(1)}, u32[]{:S(2)}, u32[]{:S(2)}) collective-permute-start(bf16[8,256]{1,0:T(8,128)(2,1)S(1)} %get-tuple-element.104), channel_id=1, source_target_pairs={{0,1},{1,2},{2,3},{3,4},{4,5},{5,6},{6,7},{7,8},{8,9},{9,10},{10,1... | collective-permute-start | bytes 12296 | tf_op jit(solution)/shard_map/ppermute | solution.py:16
  615.3 5.9 collective-permute-start.25
  617.3 4.4 collective-permute-start.26
  618.6 7.0 collective-permute-start.27
  619.9 7.1 collective-permute-start.28
  628.4 8.3 collective-permute-start.29
where the time goes:
time: 842 us; the launch traced here: 841 us
  blocking collectives  700 us (83%)
  starting transfers between devices  86.9 us (10%)
  waiting for transfers between devices  34.7 us (4%)
    psum x3, blocking collectives, on_device(): dot_sums = lax.psum(products_local, ('side', 'grp', 'dev'))  311 us
    psum x3, blocking collectives, on_device(): lax.psum(jnp.sum(remainder * remainder, axis=1), ('side', 'grp', 'dev'))  283 us
    psum x1, blocking collectives, on_device(): squares = lax.psum(jnp.sum(start * start, axis=1), ('side', 'grp', 'dev'))  106 us
    ppermute x24, starting transfers between devices, shifted(): return lax.ppermute(block, axis, route)  59.5 us
    ppermute x6, starting transfers between devices, swapped(): lax.ppermute(value, axis, [(i, i ^ 1 << distance) for i in range(lax.axis...  27.3 us
    ppermute x6, waiting for transfers between devices, swapped(): lax.ppermute(value, axis, [(i, i ^ 1 << distance) for i in range(lax.axis...  18.5 us
  transfers between devices with their start and end apart: 30, of which 15 were waited for; matrix products, arithmetic and copies ran while one was open for 0% of the time, Pallas kernels for 0%

commit v1 on v0

--- a/solution.py
+++ b/solution.py
@@ -85,7 +85,8 @@
             "jr,jrp->rp", coeffs, stacked, precision=lax.Precision.HIGHEST
         )
         rem_squares = (
-            lax.psum(jnp.sum(remainder * remainder, axis=1), ("side", "grp", "dev")) * inner_scale
+            lax.psum(lax.psum(jnp.sum(remainder * remainder, axis=1), "side"), ("grp", "dev"))
+            * inner_scale
         )
         rem_norm = jnp.sqrt(rem_squares + epsilon)
         vectors_list.append(remainder / rem_norm[:, None])

time: 842 us -> 2580 us (3.06)
  blocking collectives: 700 us -> 2450 us
    psum x3 -> x6, blocking collectives: 283 us -> 2020 us  [the longest x3 2000 us: on_device(): lax.psum(lax.psum(jnp.sum(remainder * remainder, axis=1), 'side'), ('grp'...]
where the time goes in v1:
time: 2580 us
  blocking collectives  2450 us (95%)
  starting transfers between devices  74.5 us (3%)
  waiting for transfers between devices  34 us (1%)
    psum x3, blocking collectives, on_device(): lax.psum(lax.psum(jnp.sum(remainder * remainder, axis=1), 'side'), ('grp'...  2000 us
    psum x3, blocking collectives, on_device(): dot_sums = lax.psum(products_local, ('side', 'grp', 'dev'))  327 us
    psum x1, blocking collectives, on_device(): squares = lax.psum(jnp.sum(start * start, axis=1), ('side', 'grp', 'dev'))  106 us
  transfers between devices with their start and end apart: 30, of which 15 were waited for; matrix products, arithmetic and copies ran while one was open for 0% of the time, Pallas kernels for 0%

profile of v1, /device:TPU:1, one launch (start us, length us, event | category | flops | bytes accessed | tf_op | source)
XLA Modules:
  0.0 2581.3 jit_solution(6570950832294002115)
XLA Ops:
  0.7 0.9 fusion.35
  1.6 106.1 %psum.70 = f32[8]{0:T(128)S(1)} all-reduce(f32[8]{0:T(128)S(1)} %fusion.35), channel_id=1, replica_groups=mesh['side'=2,'grp'=8,'dev'=32] {'side','grp','dev'}, use_global_device_ids=true, to_apply=%region_1.0 | all-reduce | flops 8 | bytes 64 | tf_op jit(solution)/shard_map/psum | solution.py:43
  107.8 4.7 collective-permute-start
  112.5 0.6 copy-done.4
  113.2 2.9 collective-permute-done
  116.3 2.6 collective-permute-start.1
  118.9 5.9 collective-permute-start.2
  124.8 2.4 collective-permute-start.3
  127.3 2.0 collective-permute-start.4
  129.2 2.3 collective-permute-start.5
  131.6 1.3 collective-permute-start.6
  132.9 1.3 collective-permute-start.7
  134.2 1.3 collective-permute-start.8
  136.0 3.5 collective-permute-done.7
  139.5 1.4 collective-permute-done.8
  141.5 0.6 fusion.7
  142.1 0.7 copy-done.2
  143.0 5.2 collective-permute-start.9
  148.1 3.1 collective-permute-done.9
  151.6 104.0 %psum.71 = f32[1,8]{1,0:T(1,128)S(1)} all-reduce(f32[1,8]{1,0:T(1,128)S(1)} %bitcast.209), channel_id=1, replica_groups=mesh['side'=2,'grp'=8,'dev'=32] {'side','grp','dev'}, use_global_device_ids=true, to_apply=%region_3.4 | all-reduce | flops 8 | bytes 64 | tf_op jit(solution)/shard_map/psum | solution.py:82
  255.9 7.7 psum.72
  263.6 666.1 %psum.73 = f32[8]{0:T(128)S(1)} all-reduce(f32[8]{0:T(128)S(1)} %psum.72), channel_id=1, replica_groups=mesh['side'=2,'grp'=8,'dev'=32] {'grp','dev'}, use_global_device_ids=true, to_apply=%region_6.7 | all-reduce | flops 8 | bytes 64 | tf_op jit(solution)/shard_map/psum | solution.py:88
  929.7 4.2 collective-permute-start.10
  934.0 4.0 collective-permute-done.10
  938.3 1.3 collective-permute-start.11
  939.6 1.3 collective-permute-start.12
  940.9 1.3 collective-permute-start.13
  942.2 1.9 collective-permute-start.14
  944.1 3.7 collective-permute-start.15
  947.9 1.3 collective-permute-start.16
  949.2 1.3 collective-permute-start.17
  950.5 1.3 collective-permute-start.18
  952.4 2.7 collective-permute-done.17
  955.0 1.8 collective-permute-done.18
  957.5 0.6 fusion.5
  958.3 5.0 collective-permute-start.19
  963.3 3.3 collective-permute-done.19
  967.0 110.7 %psum.74 = f32[2,8]{1,0:T(2,128)S(1)} all-reduce(f32[2,8]{1,0:T(2,128)S(1)} %get-tuple-element.81), channel_id=1, replica_groups=mesh['side'=2,'grp'=8,'dev'=32] {'side','grp','dev'}, use_global_device_ids=true, to_apply=%region_8.9 | all-reduce | flops 16 | bytes 128 | tf_op jit(solution)/shard_map/psum | solution.py:82
  1078.0 7.7 psum.75
  1085.7 666.1 %psum.76 = f32[8]{0:T(128)S(1)} all-reduce(f32[8]{0:T(128)S(1)} %psum.75), channel_id=1, replica_groups=mesh['side'=2,'grp'=8,'dev'=32] {'grp','dev'}, use_global_device_ids=true, to_apply=%region_11.12 | all-reduce | flops 8 | bytes 64 | tf_op jit(solution)/shard_map/psum | solution.py:88
  1751.9 4.8 collective-permute-start.20
  1757.3 2.9 collective-permute-done.20
  1760.5 1.3 collective-permute-start.21
  1761.8 1.3 collective-permute-start.22
  1763.1 1.3 collective-permute-start.23
  1764.4 1.9 collective-permute-start.24
  1766.3 4.0 collective-permute-start.25
  1770.3 1.3 collective-permute-start.26
  1771.6 1.3 collective-permute-start.27
  1772.9 1.3 collective-permute-start.28
  1774.8 2.7 collective-permute-done.27
  1777.5 1.8 collective-permute-done.28
  1779.9 0.6 fusion.3
  1780.7 4.4 collective-permute-start.29
  1785.1 0.7 fusion.86
  1785.8 0.7 and_reduce_fusion
  1786.6 2.4 collective-permute-done.29
  1789.4 111.8 %psum.77 = f32[3,8]{1,0:T(4,128)S(1)} all-reduce(f32[3,8]{1,0:T(4,128)S(1)} %get-tuple-element.79), channel_id=1, replica_groups=mesh['side'=2,'grp'=8,'dev'=32] {'side','grp','dev'}, use_global_device_ids=true, to_apply=%region_13.14 | all-reduce | flops 24 | bytes 192 | tf_op jit(solution)/shard_map/psum | solution.py:82
  1901.6 1.3 scatter.24
  1902.9 7.7 psum.78
  1910.7 666.1 %psum.79 = f32[8]{0:T(128)S(1)} all-reduce(f32[8]{0:T(128)S(1)} %psum.78), channel_id=1, replica_groups=mesh['side'=2,'grp'=8,'dev'=32] {'grp','dev'}, use_global_device_ids=true, to_apply=%region_16.17 | all-reduce | flops 8 | bytes 64 | tf_op jit(solution)/shard_map/psum | solution.py:88
  2576.8 0.6 maximum_bitcast_fusion
  2577.5 1.9 broadcast_select_fusion
  2579.4 1.3 scatter.26
  (98 shorter events, 8.2 us)
Async XLA Ops:
  0.6 140.8 %copy-start = (bf16[1,32,128,128]{3,2,1,0:T(8,128)(2,1)S(1)}, bf16[1,32,128,128]{3,2,1,0:T(8,128)(2,1)}, u32[]{:S(2)}) copy-start(bf16[1,32,128,128]{3,2,1,0:T(8,128)(2,1)} %param.18) | copy-start | bytes 3145732
  0.6 107.1 %copy-start.1 = (f32[1,8,256]{2,1,0:T(8,128)S(1)}, f32[1,8,256]{2,1,0:T(8,128)}, u32[]{:S(2)}) copy-start(f32[1,8,256]{2,1,0:T(8,128)} %param.17) | copy-start | bytes 24580
  107.8 8.3 collective-permute-start
  112.5 0.7 copy-start.4
  113.2 2.9 copy-start.3
  116.3 15.2 collective-permute-start.1
  118.9 14.0 collective-permute-start.2
  124.8 9.4 collective-permute-start.3
  127.3 8.3 collective-permute-start.4
  129.2 6.4 collective-permute-start.5
  131.6 4.4 collective-permute-start.6
  132.9 6.6 collective-permute-start.7
  134.2 6.6 collective-permute-start.8
  142.1 0.7 copy-start.2
  143.0 8.3 collective-permute-start.9
  929.7 8.3 collective-permute-start.10
  938.3 9.6 collective-permute-start.11
  939.6 9.6 collective-permute-start.12
  940.9 9.6 collective-permute-start.13
  942.2 9.7 collective-permute-start.14
  944.1 7.8 collective-permute-start.15
  947.9 4.5 collective-permute-start.16
  949.2 5.8 collective-permute-start.17
  950.5 6.3 collective-permute-start.18
  958.3 8.3 collective-permute-start.19
  1751.9 8.3 collective-permute-start.20
  1760.5 9.8 collective-permute-start.21
  1761.8 9.8 collective-permute-start.22
  1763.1 9.9 collective-permute-start.23
  1764.4 9.9 collective-permute-start.24
  1766.3 8.0 collective-permute-start.25
  1770.3 4.5 collective-permute-start.26
  1771.6 5.8 collective-permute-start.27
  1772.9 6.3 collective-permute-start.28
  1780.7 8.3 collective-permute-start.29
